TPU v7x, 256 devices: a whole 4x4x8 slice. The times are simulated.
256 devices in a mesh: tile: 4 (over y), proj: 16 (over x, z_hi, core), cuts: 4 (over z_lo).
Axes of the slice: x: 4, y: 4, z: 8 (z_hi: 2, z_lo: 4; z = z_hi * 4 + z_lo), core: 2. Of those that a mesh axis runs over, the one named last changes fastest.
Arguments:
- object_field: float32 [64, 2, 384, 2048], P(('proj', 'cuts'), None, None, 'tile'), may hold values from -5 to 5
- probe_field: float32 [2, 256, 256], replicated, may hold values from -6 to 6
- amplitudes: bfloat16 [64, 4, 6, 256, 256], P(('proj', 'cuts'), 'tile'), may hold values from 0 to 16
- pos_rows: int32 [64, 4, 6], P(('proj', 'cuts'), 'tile'), may hold values from 0 to 128
- pos_cols: int32 [64, 4, 6], P(('proj', 'cuts'), 'tile'), may hold values from 0 to 512
- counts: int32 [64, 4], P(('proj', 'cuts'), 'tile'), may hold values from 1 to 6, as said below
- admm_dual: float32 [64, 32, 2048], P(('proj', 'cuts'), None, 'tile'), may hold values from -4 to 4
- volume: float32 [32, 2048, 2048], P('cuts', ('tile', 'proj')), may hold values from -6 to 6
- proj_weights: bfloat16 [16, 2048, 2048], P(None, ('tile', 'proj')), may hold values from -0.125 to 0.125
- ray_weights: float32 [16, 2048], replicated, may hold values from -0.125 to 0.125
- angle_ids: int32 [64], replicated, may hold values from 0 to 15
Outputs:
- new_object: float32 [64, 2, 384, 2048], P(('proj', 'cuts'), None, None, 'tile')
- new_probe: float32 [2, 256, 256], replicated
- new_volume: float32 [32, 2048, 2048], P('cuts', ('tile', 'proj'))
Inputs may be any that keep to these rules, and one draw needn't show every extreme that they name: `counts`: every tile holds at least one live position and at most 6; exactly one tile of one projection holds 6, every other holds at most 3.
All inputs are finite; a program needn't handle non-finite values.
Results may differ from a plain program's by a relative error of at most 0.00095.
The roundings to bfloat16 on the way count: a program that leaves them out, or rounds other values in their place, can miss the bound.
Values may be sent and summed in bfloat16 or wider, within the bound.
A program may use at most 64 MiB of HBM per device.

v0:
```python
import math
import jax
import jax.numpy as jnp
from jax import lax
from jax.sharding import PartitionSpec as P

PB = 256
tomo_step = 1.0


def shifted(value, axis, steps):
    count = lax.axis_size(axis)
    leading, last = (max(0, -steps), min(count, count - steps))
    return lax.ppermute(value, axis, [(source, source + steps) for source in range(leading, last)])


def dft_tables(side):
    indices = jnp.arange(side, dtype=jnp.int32)
    products = indices[:, None] * indices[None, :] % side
    phase_angle = products.astype(jnp.float32) * (2.0 * math.pi / side)
    norm_factor = 1.0 / math.sqrt(side)
    return (
        (jnp.cos(phase_angle) * norm_factor).astype(jnp.bfloat16),
        (-jnp.sin(phase_angle) * norm_factor).astype(jnp.bfloat16),
    )


def matmul(left, right):
    return jnp.dot(left, right, preferred_element_type=jnp.float32)


def complex_matmul(left_real, left_imag, right_real, right_imag):
    out_real = matmul(left_real, right_real) - matmul(left_imag, right_imag)
    out_imag = matmul(left_real, right_imag) + matmul(left_imag, right_real)
    return (out_real, out_imag)


def patch_terms(patch_real, patch_imag, probe_real, probe_imag, amplitude, dft_real, dft_imag):
    wave_real = (probe_real * patch_real - probe_imag * patch_imag).astype(jnp.bfloat16)
    wave_imag = (probe_real * patch_imag + probe_imag * patch_real).astype(jnp.bfloat16)
    half_real, half_imag = complex_matmul(dft_real, dft_imag, wave_real, wave_imag)
    half_real = half_real.astype(jnp.bfloat16)
    half_imag = half_imag.astype(jnp.bfloat16)
    far_real, far_imag = complex_matmul(half_real, half_imag, dft_real, dft_imag)
    modulus = jnp.sqrt(far_real * far_real + far_imag * far_imag + 0.25)
    factor = amplitude.astype(jnp.float32) / modulus - 1.0
    diff_real = (far_real * factor).astype(jnp.bfloat16)
    diff_imag = (far_imag * factor).astype(jnp.bfloat16)
    conj_imag = -dft_imag
    back_half_real, back_half_imag = complex_matmul(dft_real, conj_imag, diff_real, diff_imag)
    back_half_real = back_half_real.astype(jnp.bfloat16)
    back_half_imag = back_half_imag.astype(jnp.bfloat16)
    back_real, back_imag = complex_matmul(back_half_real, back_half_imag, dft_real, conj_imag)
    object_real = probe_real * back_real + probe_imag * back_imag
    object_imag = probe_real * back_imag - probe_imag * back_real
    probe_grad_real = patch_real * back_real + patch_imag * back_imag
    probe_grad_imag = patch_real * back_imag - patch_imag * back_real
    energy = jnp.mean(patch_real * patch_real + patch_imag * patch_imag)
    return (
        jnp.stack([object_real, object_imag]),
        jnp.stack([probe_grad_real, probe_grad_imag]),
        energy,
    )


def tile_edges(values, offset):
    return shifted(values, "tile", offset)


def on_device(
    object_field,
    probe_field,
    amplitudes,
    pos_rows,
    pos_cols,
    counts,
    admm_dual,
    volume,
    proj_weights,
    ray_weights,
    angle_ids,
):
    half_side = PB // 2
    own_object = object_field[0]
    tile_cols = own_object.shape[2]
    from_left = tile_edges(own_object[:, :, tile_cols - half_side :], 1)
    from_right = tile_edges(own_object[:, :, :half_side], -1)
    extended = jnp.concatenate([from_left, own_object, from_right], axis=2)
    dft_real, dft_imag = dft_tables(PB)
    probe_real = probe_field[0]
    probe_imag = probe_field[1]
    zero_index = jnp.zeros((), jnp.int32)
    live_count = counts[0, 0]
    slot_total = amplitudes.shape[2]

    def slot_step(slot_index, state_tuple, weight):
        grad_sum, probe_sum, energy_sum = state_tuple
        anchor = (zero_index, pos_rows[0, 0, slot_index], pos_cols[0, 0, slot_index])
        object_patch = lax.dynamic_slice(extended, anchor, (2, PB, PB))
        object_part, probe_part, energy = patch_terms(
            object_patch[0],
            object_patch[1],
            probe_real,
            probe_imag,
            amplitudes[0, 0, slot_index],
            dft_real,
            dft_imag,
        )
        current = lax.dynamic_slice(grad_sum, anchor, (2, PB, PB))
        grad_sum = lax.dynamic_update_slice(grad_sum, current + weight * object_part, anchor)
        return (grad_sum, probe_sum + weight * probe_part, energy_sum + weight * energy)

    running = (
        jnp.zeros(extended.shape, jnp.float32),
        jnp.zeros((2, PB, PB), jnp.float32),
        jnp.zeros((), jnp.float32),
    )
    running = lax.fori_loop(
        0,
        slot_total,
        lambda slot_index, state_tuple: slot_step(
            slot_index, state_tuple, (slot_index < live_count).astype(jnp.float32)
        ),
        running,
    )
    grad_sum, probe_sum, energy_sum = running
    to_right_edge = tile_edges(grad_sum[:, :, :half_side], -1)
    to_left_edge = tile_edges(grad_sum[:, :, tile_cols + half_side :], 1)
    own_cells = grad_sum[:, :, half_side : half_side + tile_cols]
    own_cells = own_cells.at[:, :, :half_side].add(to_left_edge)
    own_cells = own_cells.at[:, :, tile_cols - half_side :].add(to_right_edge)
    probe_grad, energy = lax.psum((probe_sum, energy_sum), ("tile", "proj", "cuts"))
    new_probe = probe_field + probe_grad / (energy + 1e-05)
    probe_peak = jnp.max(probe_real * probe_real + probe_imag * probe_imag)
    new_object = (own_object + own_cells / (probe_peak + 1e-05))[None]
    slab_total = admm_dual.shape[1]
    first_row = (own_object.shape[1] - slab_total) // 2
    slab_values = new_object[:, 1, first_row : first_row + slab_total, :] + admm_dual
    arrived = lax.all_to_all(
        lax.all_to_all(slab_values, "proj", split_axis=2, concat_axis=0, tiled=True),
        "cuts",
        split_axis=1,
        concat_axis=0,
        tiled=True,
    )
    proj_count = lax.axis_size("proj")
    cuts_count = lax.axis_size("cuts")
    slab_dev = arrived.shape[1]
    u_share = arrived.shape[2]
    projections = proj_count * cuts_count
    arrived = arrived.reshape(cuts_count, proj_count, slab_dev, u_share).transpose(1, 0, 2, 3)
    target = (
        arrived.reshape(projections, slab_dev, u_share)
        .transpose(2, 0, 1)
        .reshape(u_share, projections * slab_dev)
    )
    angle_count = ray_weights.shape[0]
    x_share = volume.shape[1]
    width = volume.shape[2]
    onehot = (angle_ids[:, None] == jnp.arange(angle_count, dtype=jnp.int32)[None, :]).astype(
        jnp.float32
    )
    ray_table = jnp.dot(
        onehot, ray_weights, precision=lax.Precision.HIGHEST, preferred_element_type=jnp.float32
    )
    ray_sums = jnp.einsum("zxy,ay->azx", volume, ray_table, precision=lax.Precision.HIGHEST).astype(
        jnp.bfloat16
    )
    spread = onehot.astype(jnp.bfloat16)[:, :, None, None] * ray_sums[:, None, :, :]
    spread = spread.transpose(1, 3, 0, 2).reshape(angle_count * x_share, projections * slab_dev)
    weight_flat = proj_weights.reshape(angle_count * x_share, width)
    partial_term = lax.dot_general(
        weight_flat, spread, (((0,), (0,)), ((), ())), preferred_element_type=jnp.float32
    )
    row_start = lax.axis_index(("tile", "proj")) * u_share
    own_rows = lax.dynamic_slice_in_dim(partial_term, row_start, u_share, 0)
    partial_term = lax.dynamic_update_slice_in_dim(partial_term, own_rows - target, row_start, 0)
    summed = lax.psum(partial_term, ("tile", "proj"))
    residue = summed.astype(jnp.bfloat16)
    backproj = matmul(weight_flat, residue)
    backproj = backproj.reshape(angle_count, x_share, projections, slab_dev)
    back_sums = jnp.einsum("gxaz,ag->azx", backproj, onehot, precision=lax.Precision.HIGHEST)
    gradient = jnp.einsum("azx,ay->zxy", back_sums, ray_table, precision=lax.Precision.HIGHEST)
    new_volume = volume - tomo_step * gradient
    return (new_object, new_probe, new_volume)


def solution(mesh):
    in_specs = (
        P(("proj", "cuts"), None, None, "tile"),
        P(),
        P(("proj", "cuts"), "tile", None, None, None),
        P(("proj", "cuts"), "tile", None),
        P(("proj", "cuts"), "tile", None),
        P(("proj", "cuts"), "tile"),
        P(("proj", "cuts"), None, "tile"),
        P("cuts", ("tile", "proj"), None),
        P(None, ("tile", "proj"), None),
        P(),
        P(),
    )
    out_specs = (P(("proj", "cuts"), None, None, "tile"), P(), P("cuts", ("tile", "proj"), None))
    return jax.shard_map(
        on_device, mesh=mesh, in_specs=in_specs, out_specs=out_specs, check_vma=False
    )
```

profile of v0, /device:TPU:64, one launch (start us, length us, event | category | flops | bytes accessed | tf_op | source)
XLA Modules:
  0.0 1082.3 jit_solution(16087223290670484655)
XLA Ops:
  7.2 3.2 copy.38
  13.8 5.3 collective-permute-start
  20.4 3.4 fusion.127
  25.5 4.1 mul.437
  30.3 3.0 pad_maximum_fusion
  34.9 254.5 %while.23 = (s32[]{:T(128)}, f32[2,384,768]{1,2,0:T(8,128)}, f32[2,256,256]{2,1,0:T(8,128)}, f32[]{:T(128)}, s32[1,1,6]{2,1,0:T(1,128)S(1)}, /*index=5*/s32[1,1,...) while((s32[]{:T(128)}, f32[2,384,768]{1,2,0:T(8,128)}, ...), condition=%wide.region_2.3_spmd.clone.clone, body=%wide.region_0.2_spmd.clone.clone.sunk | while | flops 558956544 | bytes 22151564 | solution.py:118
  68.2 6.5 dynamic_update_slice.17
  110.5 6.5 dynamic_update_slice.17
  153.0 6.1 dynamic_update_slice.17
  195.0 6.6 dynamic_update_slice.17
  237.5 6.5 dynamic_update_slice.17
  280.0 6.5 dynamic_update_slice.17
  291.5 2.8 collective-permute-start.2
  295.6 4.3 fusion.138
  301.4 2.7 slice.97
  313.8 9.8 all-to-all-start
  323.7 79.2 %psum.22 = f32[]{:T(128)} all-reduce(f32[]{:T(128)} %get-tuple-element.384), channel_id=1, replica_groups=mesh['tile'=4,'proj'=16,'cuts'=4] {'tile','proj','cuts'}, use_global_device_ids=true, to_apply=%region_5.6 | all-reduce | flops 1 | bytes 8 | tf_op jit(solution)/shard_map/psum | solution.py:132
  405.8 6.0 all-to-all-start.1
  411.8 145.5 %all-reduce.3.cloned.1.call-done = f32[2,256,256]{2,1,0:T(8,128)} async-done(((f32[2,256,256]{2,1,0:T(8,128)}), f32[2,256,256]{2,1,0:T(8,128)}) %all-reduce.3.cloned.1.call-update) | async-done | bytes 524304 | tf_op jit(solution)/shard_map/psum | solution.py:132
  559.2 3.0 copy.48
  566.2 495.1 %all-reduce.4 = bf16[2048,512]{0,1:T(8,128)(2,1)} all-reduce(f32[2048,512]{0,1:T(8,128)} %dynamic_update_slice.13), channel_id=1, replica_groups=mesh['tile'=4,'proj'=16,'cuts'=4] {'tile','proj'}, use_global_device_ids=true, to_apply=%region_6.7 | all-reduce | flops 1048576 | bytes 6291456 | tf_op jit(solution)/shard_map/psum | solution.py:178
  1061.4 2.9 fusion.124
  1066.7 3.8 fusion.130
  1070.7 4.7 convolution_subtract_fusion.4
  (235 shorter events, 217.6 us)
Async XLA Ops:
  7.2 288.4 %copy-start = (bf16[16,32,2048]{2,1,0:T(8,128)(2,1)S(1)}, bf16[16,32,2048]{2,1,0:T(8,128)(2,1)}, u32[]{:S(2)}) copy-start(bf16[16,32,2048]{2,1,0:T(8,128)(2,1)} %param.25) | copy-start | bytes 6291460
  7.2 11.9 %copy-start.12 = (s32[64]{0:T(128)S(1)}, s32[64]{0:T(128)}, u32[]{:S(2)}) copy-start(s32[64]{0:T(128)} %param.27) | copy-start | bytes 772
  7.2 11.9 %copy-start.8 = (f32[16,2048]{1,0:T(8,128)S(1)}, f32[16,2048]{1,0:T(8,128)}, u32[]{:S(2)}) copy-start(f32[16,2048]{1,0:T(8,128)} %param.26) | copy-start | bytes 393220
  7.2 550.1 %all-reduce.3.cloned.1.call-start = ((), (), s32[]{:S(2)}) async-start(), calls=%async_computation.2 | async-start | bytes 1048576 | tf_op jit(solution)/shard_map/psum | solution.py:132
  12.5 17.9 %collective-permute-start.1 = (f32[2,384,128]{1,2,0:T(8,128)}, f32[2,384,128]{1,2,0:T(8,128)S(1)}, u32[]{:S(2)}, u32[]{:S(2)}) collective-permute-start(f32[2,384,128]{1,2,0:T(8,128)} %get-tuple-element.557), channel_id=1, source_target_pairs={{64,0},{128,64},{192,128},{65,1},{129,65},{193,129},{66,2},{130,66... | collective-permute-start | bytes 1179656 | tf_op jit(solution)/shard_map/ppermute | solution.py:14
  13.8 16.6 %collective-permute-start = (f32[2,384,128]{1,2,0:T(8,128)}, f32[2,384,128]{1,2,0:T(8,128)}, u32[]{:S(2)}, u32[]{:S(2)}) collective-permute-start(f32[2,384,128]{1,2,0:T(8,128)} %get-tuple-element.556), channel_id=1, source_target_pairs={{0,64},{64,128},{128,192},{1,65},{65,129},{129,193},{2,66},{66,130... | collective-permute-start | bytes 1179656 | tf_op jit(solution)/shard_map/ppermute | solution.py:14
  23.9 5.7 copy-start.4
  33.4 1.6 copy-start.10
  33.4 1.6 copy-start.11
  60.5 3.5 copy-start.1
  102.8 3.4 copy-start.1
  145.3 3.5 copy-start.1
  187.4 3.5 copy-start.1
  229.9 3.4 copy-start.1
  272.4 3.4 copy-start.1
  291.5 12.6 %collective-permute-start.2 = (f32[2,384,128]{1,2,0:T(8,128)}, f32[2,384,128]{1,2,0:T(8,128)}, u32[]{:S(2)}, u32[]{:S(2)}) collective-permute-start(f32[2,384,128]{1,2,0:T(8,128)} %get-tuple-element.555), channel_id=1, source_target_pairs={{0,64},{64,128},{128,192},{1,65},{65,129},{129,193},{2,66},{66,130... | collective-permute-start | bytes 1179656 | tf_op jit(solution)/shard_map/ppermute | solution.py:14
  294.3 11.9 %collective-permute-start.3 = (f32[2,384,128]{1,2,0:T(8,128)S(1)}, f32[2,384,128]{1,2,0:T(8,128)}, u32[]{:S(2)}, u32[]{:S(2)}) collective-permute-start(f32[2,384,128]{1,2,0:T(8,128)S(1)} %get-tuple-element.554), channel_id=1, source_target_pairs={{64,0},{128,64},{192,128},{65,1},{129,65},{193,129},{66,2},{130,66... | collective-permute-start | bytes 1179656 | tf_op jit(solution)/shard_map/ppermute | solution.py:14
  295.6 4.3 copy-start.9
  295.6 4.5 copy-start.5
  304.0 4.0 copy-start.2
  309.7 1.1 copy-start.3
  313.8 89.7 %all-to-all-start = ((f32[16,1,1024]{2,1,0:T(1,128)}), f32[16,1,1024]{2,1,0:T(1,128)S(1)}, u32[]{:S(2)}, u32[]{:S(2)}) async-start(f32[16,1,1024]{2,1,0:T(1,128)} %reshape.128), calls=%async_computation | async-start | bytes 131072 | tf_op jit(solution)/shard_map/all_to_all | solution.py:140
  405.8 156.4 %all-to-all-start.1 = ((f32[4,1,4096]{2,1,0:T(1,128)}), f32[4,1,4096]{2,1,0:T(1,128)S(1)}, u32[]{:S(2)}, u32[]{:S(2)}) async-start(f32[4,1,4096]{2,1,0:T(1,128)} %reshape.130), calls=%async_computation.1 | async-start | bytes 131072 | tf_op jit(solution)/shard_map/all_to_all | solution.py:139
  1066.7 4.0 copy-start.7
  (1 other events, 0.8 us)
Sparse Core Ops, SparseCore 0:
  304.2 253.0 all-reduce.2
where the time goes:
time: 1090 us; the launch traced here: 1080 us
  blocking collectives  574 us (53%)
  waiting for transfers between devices  146 us (13%)
  matrix products  141 us (13%)
  local copies, waits for them, and re-layouts  101 us (9%)
  other arithmetic  45.9 us (4%)
  loops' own time  31.6 us (3%)
  starting transfers between devices  26.6 us (2%)
  between operations  15.6 us (1%)
    psum x1, blocking collectives, on_device(): summed = lax.psum(partial_term, ('tile', 'proj'))  495 us
    psum x1, waiting for transfers between devices, on_device(): lax.psum((probe_sum, energy_sum), ('tile', 'proj', 'cuts'))  145 us
    dot_general x97, matrix products, matmul(): return jnp.dot(left, right, preferred_element_type=jnp.float32)  125 us
    psum x1, blocking collectives, on_device(): lax.psum((probe_sum, energy_sum), ('tile', 'proj', 'cuts'))  79.2 us
    dynamic_update_slice x12, local copies, waits for them, and re-layouts, slot_step(): lax.dynamic_update_slice(grad_sum, current + weight * object_part, anchor)  39.9 us
    another operation x1, loops' own time, on_device(): lax.fori_loop(0, slot_total, lambda slot_index, state_tuple: slot_step(sl...  31.6 us
  transfers between devices with their start and end apart: 7, of which 2 were waited for; matrix products, arithmetic and copies ran while one was open for 3% of the time, Pallas kernels for 0%

commit v1 on v0

--- a/solution.py
+++ b/solution.py
@@ -129,7 +129,7 @@
     own_cells = grad_sum[:, :, half_side : half_side + tile_cols]
     own_cells = own_cells.at[:, :, :half_side].add(to_left_edge)
     own_cells = own_cells.at[:, :, tile_cols - half_side :].add(to_right_edge)
-    probe_grad, energy = lax.psum((probe_sum, energy_sum), ("tile", "proj", "cuts"))
+    probe_grad, energy = lax.psum(lax.psum((probe_sum, energy_sum), ("proj", "cuts")), "tile")
     new_probe = probe_field + probe_grad / (energy + 1e-05)
     probe_peak = jnp.max(probe_real * probe_real + probe_imag * probe_imag)
     new_object = (own_object + own_cells / (probe_peak + 1e-05))[None]

time: 1090 us -> 1020 us (0.936)
  waiting for transfers between devices: 146 us -> 41.8 us
  blocking collectives: 574 us -> 605 us
    psum x1 -> x2, waiting for transfers between devices: 145 us -> 33 us  [the longest x1 33 us: on_device(): lax.psum((probe_sum, energy_sum), ('proj', 'cuts'))]
    psum x1 -> x2, blocking collectives: 79.2 us -> 136 us  [the longest x1 123 us: on_device(): lax.psum((probe_sum, energy_sum), ('proj', 'cuts'))]
    psum x1, blocking collectives: 495 us -> 469 us  [on_device(): summed = lax.psum(partial_term, ('tile', 'proj'))]
  transfers between devices with their start and end apart: 7 -> 8, of which waited for: 2 -> 4; matrix products, arithmetic and copies ran while one was open for 3% -> 4% of each run, Pallas kernels for 0% -> 0%
where the time goes in v1:
time: 1020 us; the launch traced here: 1010 us
  blocking collectives  605 us (59%)
  matrix products  141 us (14%)
  local copies, waits for them, and re-layouts  106 us (10%)
  other arithmetic  44.5 us (4%)
  waiting for transfers between devices  41.8 us (4%)
  loops' own time  30.6 us (3%)
  starting transfers between devices  27.8 us (3%)
  between operations  15.6 us (2%)
    psum x1, blocking collectives, on_device(): summed = lax.psum(partial_term, ('tile', 'proj'))  469 us
    dot_general x97, matrix products, matmul(): return jnp.dot(left, right, preferred_element_type=jnp.float32)  126 us
    psum x1, blocking collectives, on_device(): lax.psum((probe_sum, energy_sum), ('proj', 'cuts'))  123 us
    dynamic_update_slice x12, local copies, waits for them, and re-layouts, slot_step(): lax.dynamic_update_slice(grad_sum, current + weight * object_part, anchor)  39.9 us
    psum x1, waiting for transfers between devices, on_device(): lax.psum((probe_sum, energy_sum), ('proj', 'cuts'))  33 us
    another operation x1, loops' own time, on_device(): lax.fori_loop(0, slot_total, lambda slot_index, state_tuple: slot_step(sl...  30.6 us
  transfers between devices with their start and end apart: 8, of which 4 were waited for; matrix products, arithmetic and copies ran while one was open for 4% of the time, Pallas kernels for 0%

profile of v1, /device:TPU:64, one launch (start us, length us, event | category | flops | bytes accessed | tf_op | source)
XLA Modules:
  0.0 1011.9 jit_solution(4508090164317795506)
XLA Ops:
  7.2 3.2 copy.38
  13.8 5.3 collective-permute-start
  20.4 3.4 fusion.127
  31.4 257.5 %while.23 = (s32[]{:T(128)}, f32[2,384,768]{1,2,0:T(8,128)}, f32[2,256,256]{2,1,0:T(8,128)}, f32[]{:T(128)}, s32[1,1,6]{2,1,0:T(1,128)}, /*index=5*/s32[1,1,6]{2...) while((s32[]{:T(128)}, f32[2,384,768]{1,2,0:T(8,128)}, ...), condition=%wide.region_2.3_spmd.clone.clone, body=%wide.region_0.2_spmd.clone.clone.sunk | while | flops 558956544 | bytes 22151564 | solution.py:118
  65.1 6.5 dynamic_update_slice.17
  107.9 6.5 dynamic_update_slice.17
  150.9 6.1 dynamic_update_slice.17
  193.5 6.5 dynamic_update_slice.17
  236.5 6.5 dynamic_update_slice.17
  279.4 6.5 dynamic_update_slice.17
  291.0 4.4 collective-permute-start.2
  298.4 3.4 mul.437
  314.0 9.9 all-to-all-start
  324.0 3.2 fusion.138
  327.2 6.8 all-to-all-done
  336.2 5.2 all-to-all-start.1
  341.5 123.2 %psum.37 = f32[]{:T(128)} all-reduce(f32[]{:T(128)} %get-tuple-element.384), channel_id=1, replica_groups=mesh['tile'=4,'proj'=16,'cuts'=4] {'proj','cuts'}, use_global_device_ids=true, to_apply=%region_6.7 | all-reduce | flops 1 | bytes 8 | tf_op jit(solution)/shard_map/psum | solution.py:132
  464.7 12.3 %psum.38 = f32[]{:T(128)} all-reduce(f32[]{:T(128)} %psum.37), channel_id=1, replica_groups=mesh['tile'=4,'proj'=16,'cuts'=4] {'tile'}, use_global_device_ids=true, to_apply=%region_7.8 | all-reduce | flops 1 | bytes 8 | tf_op jit(solution)/shard_map/psum | solution.py:132
  477.7 33.0 %all-reduce.4.cloned.1.call-done = f32[2,256,256]{2,1,0:T(8,128)} async-done(((f32[2,256,256]{2,1,0:T(8,128)}), f32[2,256,256]{2,1,0:T(8,128)}) %all-reduce.4.cloned.1.call-update) | async-done | bytes 524304 | tf_op jit(solution)/shard_map/psum | solution.py:132
  517.7 469.1 %all-reduce.7 = bf16[2048,512]{0,1:T(8,128)(2,1)} all-reduce(f32[2048,512]{0,1:T(8,128)} %dynamic_update_slice.13), channel_id=1, replica_groups=mesh['tile'=4,'proj'=16,'cuts'=4] {'tile','proj'}, use_global_device_ids=true, to_apply=%region_8.9 | all-reduce | flops 1048576 | bytes 6291456 | tf_op jit(solution)/shard_map/psum | solution.py:178
  986.8 3.9 fusion.124
  990.7 3.8 reshape.122
  994.5 3.8 fusion.130
  998.4 4.7 convolution_subtract_fusion.4
  (235 shorter events, 228.3 us)
Async XLA Ops:
  7.2 316.8 %copy-start = (bf16[16,32,2048]{2,1,0:T(8,128)(2,1)S(1)}, bf16[16,32,2048]{2,1,0:T(8,128)(2,1)}, u32[]{:S(2)}) copy-start(bf16[16,32,2048]{2,1,0:T(8,128)(2,1)} %param.25) | copy-start | bytes 6291460
  7.2 12.0 %copy-start.8 = (f32[16,2048]{1,0:T(8,128)S(1)}, f32[16,2048]{1,0:T(8,128)}, u32[]{:S(2)}) copy-start(f32[16,2048]{1,0:T(8,128)} %param.26) | copy-start | bytes 393220
  7.2 12.0 %copy-start.9 = (s32[64]{0:T(128)S(1)}, s32[64]{0:T(128)}, u32[]{:S(2)}) copy-start(s32[64]{0:T(128)} %param.27) | copy-start | bytes 772
  12.4 11.6 %copy-start.4 = (f32[2,256,256]{2,1,0:T(8,128)S(1)}, f32[2,256,256]{2,1,0:T(8,128)}, u32[]{:S(2)}) copy-start(f32[2,256,256]{2,1,0:T(8,128)} %param.18) | copy-start | bytes 1572868
  12.4 13.1 %collective-permute-start.1 = (f32[2,384,128]{1,2,0:T(8,128)}, f32[2,384,128]{1,2,0:T(8,128)S(1)}, u32[]{:S(2)}, u32[]{:S(2)}) collective-permute-start(f32[2,384,128]{1,2,0:T(8,128)} %get-tuple-element.557), channel_id=1, source_target_pairs={{64,0},{128,64},{192,128},{65,1},{129,65},{193,129},{66,2},{130,66... | collective-permute-start | bytes 1179656 | tf_op jit(solution)/shard_map/ppermute | solution.py:14
  13.8 12.9 %collective-permute-start = (f32[2,384,128]{1,2,0:T(8,128)}, f32[2,384,128]{1,2,0:T(8,128)}, u32[]{:S(2)}, u32[]{:S(2)}) collective-permute-start(f32[2,384,128]{1,2,0:T(8,128)} %get-tuple-element.556), channel_id=1, source_target_pairs={{0,64},{64,128},{128,192},{1,65},{65,129},{129,193},{2,66},{66,130... | collective-permute-start | bytes 1179656 | tf_op jit(solution)/shard_map/ppermute | solution.py:14
  19.6 0.8 copy-start.6
  57.5 3.4 copy-start.1
  100.3 3.5 copy-start.1
  143.3 3.4 copy-start.1
  185.8 3.5 copy-start.1
  228.8 3.4 copy-start.1
  271.8 3.5 copy-start.1
  291.0 14.8 %collective-permute-start.2 = (f32[2,384,128]{1,2,0:T(8,128)}, f32[2,384,128]{1,2,0:T(8,128)}, u32[]{:S(2)}, u32[]{:S(2)}) collective-permute-start(f32[2,384,128]{1,2,0:T(8,128)} %get-tuple-element.555), channel_id=1, source_target_pairs={{0,64},{64,128},{128,192},{1,65},{65,129},{129,193},{2,66},{66,130... | collective-permute-start | bytes 1179656 | tf_op jit(solution)/shard_map/ppermute | solution.py:14
  295.4 7.4 copy-start.5
  295.4 11.5 %collective-permute-start.3 = (f32[2,384,128]{1,2,0:T(8,128)}, f32[2,384,128]{1,2,0:T(8,128)}, u32[]{:S(2)}, u32[]{:S(2)}) collective-permute-start(f32[2,384,128]{1,2,0:T(8,128)} %get-tuple-element.554), channel_id=1, source_target_pairs={{64,0},{128,64},{192,128},{65,1},{129,65},{193,129},{66,2},{130,66... | collective-permute-start | bytes 1179656 | tf_op jit(solution)/shard_map/ppermute | solution.py:14
  304.1 3.9 copy-start.2
  308.2 1.1 copy-start.3
  314.0 20.0 %all-to-all-start = ((f32[16,1,1024]{2,1,0:T(1,128)}), f32[16,1,1024]{2,1,0:T(1,128)S(1)}, u32[]{:S(2)}, u32[]{:S(2)}) async-start(f32[16,1,1024]{2,1,0:T(1,128)} %reshape.128), calls=%async_computation | async-start | bytes 131072 | tf_op jit(solution)/shard_map/all_to_all | solution.py:140
  323.9 186.7 %all-reduce.4.cloned.1.call-start = ((), (), s32[]{:S(2)}) async-start(), calls=%async_computation.2 | async-start | bytes 1048576 | tf_op jit(solution)/shard_map/psum | solution.py:132
  327.2 14.2 %copy-start.10 = (s32[64]{0:T(128)S(1)}, s32[64]{0:T(128)}, u32[]{:S(2)}) copy-start(s32[64]{0:T(128)} %param.27) | copy-start | bytes 772
  336.2 177.5 %all-to-all-start.1 = ((f32[4,1,4096]{2,1,0:T(1,128)}), f32[4,1,4096]{2,1,0:T(1,128)S(1)}, u32[]{:S(2)}, u32[]{:S(2)}) async-start(f32[4,1,4096]{2,1,0:T(1,128)} %reshape.130), calls=%async_computation.1 | async-start | bytes 131072 | tf_op jit(solution)/shard_map/all_to_all | solution.py:139
  341.4 661.7 %all-reduce.6.cloned.1.call-start = ((), (), s32[]{:S(2)}) async-start(), calls=%async_computation.3 | async-start | bytes 1048576 | tf_op jit(solution)/shard_map/psum | solution.py:132
  994.5 4.0 copy-start.7
Sparse Core Ops, SparseCore 0:
  328.8 181.7 all-reduce.3
  513.0 50.4 all-reduce.5
